TPU v7x, 256 devices: a whole 4x4x8 slice. The times are simulated.
256 devices in a mesh: ctx: 8 (over z), chan: 32 (over x, y, core).
Axes of the slice: x: 4, y: 4, z: 8, core: 2. Of those that a mesh axis runs over, the one named last changes fastest.
Arguments:
- query_rows: bfloat16 [2048, 8192], P('ctx', 'chan'), may hold values from -6 to 6
- key_rows: bfloat16 [2048, 8192], P('ctx', 'chan'), may hold values from -6 to 6
- value_rows: bfloat16 [2048, 8192], P('ctx', 'chan'), may hold values from -6 to 6
- short_taps: float32 [3, 3, 8192], P(None, None, 'chan'), may hold values from -3 to 3
- long_filter: bfloat16 [2048, 8192], P('ctx', 'chan'), may hold values from -4 to 4
- direction: bfloat16 [2048, 8192], P('ctx', 'chan'), may hold values from -4 to 4
- w_out: bfloat16 [8192, 8192], P('chan'), may hold values from -0.125 to 0.125
- target: bfloat16 [2048, 8192], P('ctx'), may hold values from -6 to 6
Outputs:
- grad_filter: float32 [2048, 8192], P('ctx', 'chan')
- hvp_filter: float32 [2048, 8192], P('ctx', 'chan')
All inputs are finite; a program needn't handle non-finite values.
Results may differ from a plain program's by a relative error of at most 0.033.
Values may be sent and summed in bfloat16 or wider, within the bound.
A program may use at most 128 MiB of HBM per device.

v0:
```python
import math
import jax
import jax.numpy as jnp
from jax import lax
from jax.sharding import PartitionSpec as P


def passed_along(value, axis, steps):
    count = lax.axis_size(axis)
    initial, last = (max(0, -steps), min(count, count - steps))
    return lax.ppermute(value, axis, [(source, source + steps) for source in range(initial, last)])


def short_conv(current, earlier, coeffs):
    extended = jnp.concatenate([earlier.astype(jnp.float32), current.astype(jnp.float32)], axis=0)
    length = current.shape[0]
    return (
        coeffs[0] * extended[2 : 2 + length]
        + coeffs[1] * extended[1 : 1 + length]
        + coeffs[2] * extended[0:length]
    )


def depthwise(window, kernel):
    result = lax.conv_general_dilated(
        window[None],
        kernel[:, None, :],
        (1,),
        "VALID",
        dimension_numbers=("NHC", "HIO", "NHC"),
        feature_group_count=window.shape[1],
        preferred_element_type=jnp.float32,
    )
    return result[0]


def paired(window, first_kernel, second_kernel):
    return jax.vmap(lambda kernel: depthwise(window, kernel))(
        jnp.stack([first_kernel, second_kernel])
    )


def on_device(query_rows, key_rows, value_rows, short_taps, long_filter, direction, w_out, target):
    block_len = query_rows.shape[0]
    chan_width = query_rows.shape[1]
    earlier = passed_along(
        (query_rows[block_len - 2 :], key_rows[block_len - 2 :], value_rows[block_len - 2 :]),
        "ctx",
        1,
    )
    taps_all, dir_all = (
        lax.all_gather(long_filter, "ctx", axis=0, tiled=True),
        lax.all_gather(direction, "ctx", axis=0, tiled=True),
    )
    gate_in = short_conv(query_rows, earlier[0], short_taps[0])
    key_short = short_conv(key_rows, earlier[1], short_taps[1])
    value_short = short_conv(value_rows, earlier[2], short_taps[2])
    mixed_rows = (key_short * value_short).astype(jnp.bfloat16)
    history = lax.all_gather(mixed_rows, "ctx", axis=0, tiled=True)
    seq_total = history.shape[0]
    my_block = lax.axis_index("ctx")
    padded = jnp.concatenate([jnp.zeros((block_len, chan_width), jnp.bfloat16), history], axis=0)

    def window_at(distance):
        return lax.dynamic_slice_in_dim(padded, distance * block_len + 1, 2 * block_len - 1, 0)

    def forward_step(tap_block, running):
        window = window_at(my_block - tap_block)
        taps_here = lax.dynamic_slice_in_dim(taps_all, tap_block * block_len, block_len, 0)[::-1]
        dirs_here = lax.dynamic_slice_in_dim(dir_all, tap_block * block_len, block_len, 0)[::-1]
        return running + paired(window, taps_here, dirs_here)

    convolved = lax.fori_loop(
        0, my_block + 1, forward_step, jnp.zeros((2, block_len, chan_width), jnp.float32)
    )
    gated_rows = (gate_in * convolved[0]).astype(jnp.bfloat16)
    gated_dir = (gate_in * convolved[1]).astype(jnp.bfloat16)
    stacked = jnp.concatenate([gated_rows, gated_dir], axis=0)
    scaling = 1.0 / math.sqrt(seq_total)
    summed = lax.psum_scatter(
        lax.dot_general(
            w_out, stacked, (((0,), (1,)), ((), ())), preferred_element_type=jnp.float32
        ).astype(jnp.bfloat16),
        "chan",
        scatter_dimension=0,
        tiled=True,
    ).astype(jnp.float32)
    column_start = lax.axis_index("chan") * chan_width
    target_mine = (
        lax.dynamic_slice_in_dim(target, column_start, chan_width, 1).astype(jnp.float32).T
    )
    bent_out = jnp.tanh(summed[:, :block_len] - target_mine)
    cot_grad = (scaling * bent_out).astype(jnp.bfloat16)
    cot_hvp = (scaling * (1.0 - bent_out * bent_out) * summed[:, block_len:]).astype(jnp.bfloat16)
    cotangent = jnp.concatenate([cot_grad, cot_hvp], axis=1)
    backward = jnp.dot(
        w_out,
        lax.all_gather(cotangent, "chan", axis=0, tiled=True),
        preferred_element_type=jnp.float32,
    )
    back_grad = backward[:, :block_len].T
    back_hvp = backward[:, block_len:].T
    dz_grad = (gate_in * back_grad).astype(jnp.bfloat16)
    dz_hvp = (gate_in * back_hvp).astype(jnp.bfloat16)

    def backward_step(tap_block, running):
        window = window_at(my_block - tap_block)
        pair = paired(window, dz_grad, dz_hvp)[:, ::-1]
        placed = jnp.concatenate([pair[0], pair[1]], axis=1)
        return lax.dynamic_update_slice_in_dim(running, placed, tap_block * block_len, 0)

    tap_terms = lax.fori_loop(
        0, my_block + 1, backward_step, jnp.zeros((seq_total, 2 * chan_width), jnp.float32)
    )
    shares = lax.psum_scatter(
        tap_terms.astype(jnp.bfloat16), "ctx", scatter_dimension=0, tiled=True
    ).astype(jnp.float32)
    return (shares[:, :chan_width], shares[:, chan_width:])


def solution(mesh):
    in_specs = (
        P("ctx", "chan"),
        P("ctx", "chan"),
        P("ctx", "chan"),
        P(None, None, "chan"),
        P("ctx", "chan"),
        P("ctx", "chan"),
        P("chan", None),
        P("ctx", None),
    )
    out_specs = (P("ctx", "chan"), P("ctx", "chan"))
    return jax.shard_map(
        on_device, mesh=mesh, in_specs=in_specs, out_specs=out_specs, check_vma=False
    )
```

profile of v0, /device:TPU:2, one launch (start us, length us, event | category | flops | bytes accessed | tf_op | source)
XLA Modules:
  0.0 615.9 jit_solution(8180843435490185184)
XLA Ops:
  7.2 0.7 slice.125
  7.9 3.8 collective-permute-start
  11.7 0.7 slice.131
  12.4 3.8 collective-permute-start.1
  16.2 1.5 fusion.41
  17.7 0.9 convert_element_type.55
  18.6 0.9 convert_element_type.57
  19.6 0.8 fusion.14
  20.5 0.7 all-gather.7.cloned.1.call-update
  22.0 0.7 slice.137
  22.7 3.8 collective-permute-start.2
  26.5 1.6 convert_element_type.60
  28.7 31.8 %all-gather.5.cloned.1.call-done = bf16[2048,256]{1,0:T(8,128)(2,1)} async-done(((bf16[256,256]{1,0:T(8,128)(2,1)}), bf16[2048,256]{1,0:T(8,128)(2,1)}) %all-gather.5.cloned.1.call-update) | async-done | bytes 1048592 | tf_op jit(solution)/shard_map/all_gather | solution.py:59
  60.6 1.3 concatenate.26
  61.9 37.3 %all-gather.7.cloned.1.call-done = bf16[2048,256]{1,0:T(8,128)(2,1)} async-done(((bf16[256,256]{1,0:T(8,128)(2,1)}), bf16[2048,256]{1,0:T(8,128)(2,1)}) %all-gather.7.cloned.1.call-update) | async-done | bytes 1048592 | tf_op jit(solution)/shard_map/all_gather | solution.py:52
  99.2 38.6 %all-gather.9.cloned.1.call-done = bf16[2048,256]{1,0:T(8,128)(2,1)} async-done(((bf16[256,256]{1,0:T(8,128)(2,1)}), bf16[2048,256]{1,0:T(8,128)(2,1)}) %all-gather.9.cloned.1.call-update) | async-done | bytes 1048592 | tf_op jit(solution)/shard_map/all_gather | solution.py:53
  138.0 15.6 %while.24 = (s32[]{:T(128)}, f32[2,256,256]{2,0,1:T(2,128)S(1)}, s32[]{:T(128)}, s32[]{:T(128)}, bf16[2304,256]{1,0:T(8,128)(2,1)S(1)}, /*index=5*/bf16[2048,256...) while((s32[]{:T(128)}, f32[2,256,256]{2,0,1:T(2,128)S(1)}, ...), condition=%wide.region_1.0_spmd, body=%wide.region_0.0_spmd.sunk | while | flops 67371016 | bytes 4717297 | solution.py:73
  138.0 1.0 constant_dynamic-slice_fusion.3
  139.6 13.5 %convolution_bitcast_fusion.5 = f32[2,1,256,256]{3,1,0,2:T(1,128)S(1)} fusion(bf16[256,1,256,2]{2,0,3,1:T(8,128)(2,1)S(1)} %maximum_bitcast_fusion.2, bf16[1,511,256,1]{2,1,3,0:T(8,128)(2,1)S(1)} %dynamic-slice_bitcast_fusion.4), kind=kOutput, calls=%fused_computation.clone.1 | convolution fusion | flops 67108864 | bytes 1048064 | tf_op jit(solution)/shard_map/convolution.6
  153.9 7.8 %fusion.4 = bf16[8192,512]{0,1:T(8,128)(2,1)} fusion(bf16[256,8192]{1,0:T(8,128)(2,1)} %param.18, bf16[256,256]{1,0:T(8,128)(2,1)S(1)} %fusion.26, bf16[256,256]{1,0:T(8,128)(2,1)S(1)} %get-tuple-element.225), kind=kOutput, calls=%fused_computation.17 | convolution fusion | flops 2152202240 | bytes 12845056 | tf_op jit(solution)/shard_map/dot_general | solution.py:81
  161.8 206.3 %reduce-scatter.3.cloned.1.call-done = bf16[256,512]{0,1:T(8,128)(2,1)} async-done(((bf16[8192,512]{0,1:T(8,128)(2,1)}), bf16[256,512]{0,1:T(8,128)(2,1)}) %reduce-scatter.3.cloned.1.call-update) | async-done | bytes 262160 | tf_op jit(solution)/shard_map/reduce_scatter | solution.py:80
  368.0 1.0 convert_element_type.66
  369.0 1.0 multiply_convert_fusion
  370.0 0.7 pad_maximum_fusion.3
  371.0 63.1 %all-gather.11.cloned.1.call-done = bf16[8192,512]{0,1:T(8,128)(2,1)} async-done(((bf16[256,512]{0,1:T(8,128)(2,1)}), bf16[8192,512]{0,1:T(8,128)(2,1)}) %all-gather.11.cloned.1.call-update) | async-done | bytes 8388624 | tf_op jit(solution)/shard_map/all_gather | solution.py:98
  434.1 6.9 %convolution_bitcast_fusion.2 = f32[256,512]{0,1:T(8,128)S(1)} fusion(bf16[8192,512]{0,1:T(8,128)(2,1)} %all-gather.11.cloned.1.call-done, bf16[256,8192]{1,0:T(8,128)(2,1)} %param.18), kind=kOutput, calls=%fused_computation.18 | convolution fusion | flops 2147483648 | bytes 13107200 | tf_op jit(solution)/shard_map/dot_general | solution.py:96
  441.4 1.5 broadcast_in_dim.21
  442.9 15.5 %while.25 = (s32[]{:T(128)}, bf16[2048,512]{1,0:T(8,128)(2,1)}, s32[]{:T(128)}, s32[]{:T(128)}, bf16[2304,256]{1,0:T(8,128)(2,1)S(1)}, /*index=5*/bf16[2,256,256...) while((s32[]{:T(128)}, bf16[2048,512]{1,0:T(8,128)(2,1)}, ...), condition=%wide.region_4.0_spmd, body=%wide.region_3.0_spmd.sunk | while | flops 67633160 | bytes 3406569 | solution.py:112
  442.9 13.6 %convolution_bitcast_fusion.6 = bf16[2,1,256,256]{3,1,0,2:T(2,128)(2,1)S(1)} fusion(bf16[256,1,256,2]{2,3,0,1:T(2,128)(2,1)S(1)} %bitcast.127, bf16[1,511,256,1]{2,1,3,0:T(8,128)(2,1)S(1)} %dynamic-slice_bitcast_fusion.5), kind=kOutput, calls=%fused_computation.8.clone.1 | convolution fusion | flops 67108864 | bytes 785920 | tf_op jit(solution)/shard_map/convolution.7
  457.6 0.7 maximum_dynamic-update-slice_fusion.2
  458.4 148.9 %reduce-scatter.5.cloned.1.call-done = bf16[256,512]{1,0:T(8,128)(2,1)} async-done(((bf16[2048,512]{1,0:T(8,128)(2,1)}), bf16[256,512]{1,0:T(8,128)(2,1)}) %reduce-scatter.5.cloned.1.call-update) | async-done | bytes 262160 | tf_op jit(solution)/shard_map/reduce_scatter | solution.py:115
  607.2 1.8 fusion.40
  (45 shorter events, 4.6 us)
Async XLA Ops:
  7.2 53.4 %all-gather.5.cloned.1.call-start = ((), (), s32[]{:S(2)}) async-start(), calls=%async_computation.2 | async-start | bytes 1179648 | tf_op jit(solution)/shard_map/all_gather | solution.py:59
  7.9 11.6 %collective-permute-start = (bf16[2,256]{1,0:T(2,128)(2,1)S(1)}, bf16[2,256]{1,0:T(2,128)(2,1)S(1)}, u32[]{:S(2)}, u32[]{:S(2)}) collective-permute-start(bf16[2,256]{1,0:T(2,128)(2,1)S(1)} %slice.125), channel_id=1, source_target_pairs={{0,32},{32,64},{64,96},{96,128},{128,160},{160,192},{192,224},{1,3... | collective-permute-start | bytes 3080 | tf_op jit(solution)/shard_map/ppermute | solution.py:11
  12.4 7.2 %collective-permute-start.1 = (bf16[2,256]{1,0:T(2,128)(2,1)S(1)}, bf16[2,256]{1,0:T(2,128)(2,1)S(1)}, u32[]{:S(2)}, u32[]{:S(2)}) collective-permute-start(bf16[2,256]{1,0:T(2,128)(2,1)S(1)} %slice.131), channel_id=1, source_target_pairs={{0,32},{32,64},{64,96},{96,128},{128,160},{160,192},{192,224},{1,3... | collective-permute-start | bytes 3080 | tf_op jit(solution)/shard_map/ppermute | solution.py:11
  20.4 78.7 %all-gather.7.cloned.1.call-start = ((), (), s32[]{:S(2)}) async-start(), calls=%async_computation.3 | async-start | bytes 1179648 | tf_op jit(solution)/shard_map/all_gather | solution.py:52
  21.2 116.6 %all-gather.9.cloned.1.call-start = ((), (), s32[]{:S(2)}) async-start(), calls=%async_computation.4 | async-start | bytes 1179648 | tf_op jit(solution)/shard_map/all_gather | solution.py:53
  21.9 346.1 %reduce-scatter.3.cloned.1.call-start = ((), (), s32[]{:S(2)}) async-start(), calls=%async_computation.5 | async-start | bytes 8650752 | tf_op jit(solution)/shard_map/reduce_scatter | solution.py:80
  22.7 5.5 collective-permute-start.2
  138.0 15.7 %copy-start = (f32[256,256]{1,0:T(8,128)S(1)}, f32[256,256]{1,0:T(8,128)}, u32[]{:S(2)}) copy-start(f32[256,256]{1,0:T(8,128)} %convert_element_type.60) | copy-start | bytes 786436
  138.0 15.7 %copy-start.1 = (f32[2,256]{1,0:T(2,128)S(1)}, f32[2,256]{1,0:T(2,128)}, u32[]{:S(2)}) copy-start(f32[2,256]{1,0:T(2,128)} %convert_element_type.61) | copy-start | bytes 6148
  138.0 15.7 %copy-start.2 = (f32[1,1,256]{2,1,0:T(1,128)S(1)}, f32[1,1,256]{2,1,0:T(1,128)}, u32[]{:S(2)}) copy-start(f32[1,1,256]{2,1,0:T(1,128)} %get-tuple-element.237) | copy-start | bytes 3076
  138.0 15.7 %copy-start.3 = (f32[1,1,256]{2,1,0:T(1,128)S(1)}, f32[1,1,256]{2,1,0:T(1,128)}, u32[]{:S(2)}) copy-start(f32[1,1,256]{2,1,0:T(1,128)} %get-tuple-element.244) | copy-start | bytes 3076
  138.0 15.7 %copy-start.4 = (f32[1,1,256]{2,1,0:T(1,128)S(1)}, f32[1,1,256]{2,1,0:T(1,128)}, u32[]{:S(2)}) copy-start(f32[1,1,256]{2,1,0:T(1,128)} %get-tuple-element.245) | copy-start | bytes 3076
  161.7 272.4 %all-gather.11.cloned.1.call-start = ((), (), s32[]{:S(2)}) async-start(), calls=%async_computation.6 | async-start | bytes 8650752 | tf_op jit(solution)/shard_map/all_gather | solution.py:98
  370.8 236.5 %reduce-scatter.5.cloned.1.call-start = ((), (), s32[]{:S(2)}) async-start(), calls=%async_computation.7 | async-start | bytes 2359296 | tf_op jit(solution)/shard_map/reduce_scatter | solution.py:115
Sparse Core Ops, SparseCore 0:
  20.6 39.9 all-gather.4
  62.4 36.7 all-gather.6
  101.0 36.7 all-gather.8
  161.8 206.1 reduce-scatter.2
  370.9 63.1 all-gather.10
  458.5 148.7 reduce-scatter.4
where the time goes:
time: 616 us
  waiting for transfers between devices  527 us (86%)
  matrix products  41.8 us (7%)
  between operations  14.3 us (2%)
  starting transfers between devices  11.9 us (2%)
  local copies, waits for them, and re-layouts  11.1 us (2%)
  other arithmetic  9.17 us (1%)
    reduce_scatter x1, waiting for transfers between devices, on_device(): lax.psum_scatter(lax.dot_general(w_out, stacked, (((0,), (1,)), ((), ()))...  206 us
    reduce_scatter x1, waiting for transfers between devices, on_device(): lax.psum_scatter(tap_terms.astype(jnp.bfloat16), 'ctx', scatter_dimension...  149 us
    all_gather x1, waiting for transfers between devices, on_device(): lax.all_gather(cotangent, 'chan', axis=0, tiled=True)  63.1 us
    all_gather x1, waiting for transfers between devices, on_device(): lax.all_gather(direction, 'ctx', axis=0, tiled=True)  38.6 us
    all_gather x1, waiting for transfers between devices, on_device(): lax.all_gather(long_filter, 'ctx', axis=0, tiled=True)  37.3 us
    all_gather x1, waiting for transfers between devices, on_device(): history = lax.all_gather(mixed_rows, 'ctx', axis=0, tiled=True)  31.8 us
    another operation x2, matrix products  27.1 us
  transfers between devices with their start and end apart: 9, of which 6 were waited for; matrix products, arithmetic and copies ran while one was open for 1% of the time, Pallas kernels for 0%

commit v1 on v0

--- a/solution.py
+++ b/solution.py
@@ -56,7 +56,13 @@
     key_short = short_conv(key_rows, earlier[1], short_taps[1])
     value_short = short_conv(value_rows, earlier[2], short_taps[2])
     mixed_rows = (key_short * value_short).astype(jnp.bfloat16)
-    history = lax.all_gather(mixed_rows, "ctx", axis=0, tiled=True)
+    axis_n = jax.lax.psum(1, "ctx")
+    trail = []
+    for dev_j in range(mixed_rows.ndim):
+        trail.append(axis_n if dev_j == 0 else 1)
+    history = jax.lax.all_to_all(
+        jnp.tile(mixed_rows, trail), axis_name="ctx", split_axis=0, concat_axis=0, tiled=True
+    )
     seq_total = history.shape[0]
     my_block = lax.axis_index("ctx")
     padded = jnp.concatenate([jnp.zeros((block_len, chan_width), jnp.bfloat16), history], axis=0)

time: 616 us -> 580 us (0.942)
  waiting for transfers between devices: 527 us -> 486 us
  starting transfers between devices: 11.9 us -> 19 us
    all_gather x1, waiting for transfers between devices: 37.3 us -> 0.02 us  [on_device(): lax.all_gather(long_filter, 'ctx', axis=0, tiled=True)]
    all_gather x1 -> x0, waiting for transfers between devices: 31.8 us -> none  [on_device(): history = lax.all_gather(mixed_rows, 'ctx', axis=0, tiled=True)]
    ppermute x3, waiting for transfers between devices: 0.01 us -> 22.2 us  [passed_along(): lax.ppermute(value, axis, [(source, source + steps) for source in range(i...]
    all_to_all x0 -> x1, starting transfers between devices: none -> 7.07 us  [on_device(): jax.lax.all_to_all(jnp.tile(mixed_rows, trail), axis_name='ctx', split_ax...]
where the time goes in v1:
time: 580 us; the launch traced here: 579 us
  waiting for transfers between devices  486 us (84%)
  matrix products  41.8 us (7%)
  starting transfers between devices  19 us (3%)
  between operations  14 us (2%)
  local copies, waits for them, and re-layouts  10.3 us (2%)
  other arithmetic  7.59 us (1%)
    reduce_scatter x1, waiting for transfers between devices, on_device(): lax.psum_scatter(lax.dot_general(w_out, stacked, (((0,), (1,)), ((), ()))...  206 us
    reduce_scatter x1, waiting for transfers between devices, on_device(): lax.psum_scatter(tap_terms.astype(jnp.bfloat16), 'ctx', scatter_dimension...  149 us
    all_gather x1, waiting for transfers between devices, on_device(): lax.all_gather(cotangent, 'chan', axis=0, tiled=True)  63.1 us
    all_gather x1, waiting for transfers between devices, on_device(): lax.all_gather(direction, 'ctx', axis=0, tiled=True)  39.4 us
    another operation x2, matrix products  27.1 us
    ppermute x3, waiting for transfers between devices, passed_along(): lax.ppermute(value, axis, [(source, source + steps) for source in range(i...  22.2 us
  transfers between devices with their start and end apart: 9, of which 6 were waited for; matrix products, arithmetic and copies ran while one was open for 1% of the time, Pallas kernels for 0%

profile of v1, /device:TPU:2, one launch (start us, length us, event | category | flops | bytes accessed | tf_op | source)
XLA Modules:
  0.0 579.1 jit_solution(885201320377437420)
XLA Ops:
  7.2 0.7 all-gather.4.cloned.1.call-update
  7.9 0.7 slice.125
  8.6 3.8 collective-permute-start
  12.4 0.7 slice.131
  13.1 3.8 collective-permute-start.1
  16.9 1.4 fusion.41
  18.4 0.9 convert_element_type.55
  19.3 0.9 convert_element_type.57
  20.5 1.1 tile.2
  21.5 7.1 %all-to-all-start = ((bf16[8,256,256]{2,1,0:T(8,128)(2,1)}), bf16[8,256,256]{2,1,0:T(8,128)(2,1)S(1)}, u32[]{:S(2)}, u32[]{:S(2)}) async-start(bf16[8,256,256]{2,1,0:T(8,128)(2,1)} %tile.2), calls=%async_computation | async-start | bytes 2097152 | tf_op jit(solution)/shard_map/all_to_all | solution.py:63
  28.6 0.7 all-gather.6.cloned.1.call-update
  29.4 3.9 collective-permute-start.2
  33.3 0.7 convert_element_type.60
  34.0 22.2 %collective-permute-done.2 = bf16[2,256]{1,0:T(2,128)(2,1)S(1)} collective-permute-done((bf16[2,256]{1,0:T(2,128)(2,1)S(1)}, bf16[2,256]{1,0:T(2,128)(2,1)S(1)}, u32[]{:S(2)}, u32[]{:S(2)}) %collective-permute-start.2) | collective-permute-done | bytes 1056 | tf_op jit(solution)/shard_map/ppermute | solution.py:11
  56.8 5.0 all-to-all-done
  61.9 39.4 %all-gather.6.cloned.1.call-done = bf16[2048,256]{1,0:T(8,128)(2,1)} async-done(((bf16[256,256]{1,0:T(8,128)(2,1)}), bf16[2048,256]{1,0:T(8,128)(2,1)}) %all-gather.6.cloned.1.call-update) | async-done | bytes 1048592 | tf_op jit(solution)/shard_map/all_gather | solution.py:53
  101.5 15.6 %while.24 = (s32[]{:T(128)}, f32[2,256,256]{2,0,1:T(2,128)S(1)}, s32[]{:T(128)}, s32[]{:T(128)}, bf16[2304,256]{1,0:T(8,128)(2,1)S(1)}, /*index=5*/bf16[2048,256...) while((s32[]{:T(128)}, f32[2,256,256]{2,0,1:T(2,128)S(1)}, ...), condition=%wide.region_1.0_spmd, body=%wide.region_0.0_spmd.sunk | while | flops 67371016 | bytes 4717297 | solution.py:79
  101.5 1.0 constant_dynamic-slice_fusion.3
  103.1 13.5 %convolution_bitcast_fusion.5 = f32[2,1,256,256]{3,1,0,2:T(1,128)S(1)} fusion(bf16[256,1,256,2]{2,0,3,1:T(8,128)(2,1)S(1)} %maximum_bitcast_fusion.2, bf16[1,511,256,1]{2,1,3,0:T(8,128)(2,1)S(1)} %dynamic-slice_bitcast_fusion.4), kind=kOutput, calls=%fused_computation.clone.1 | convolution fusion | flops 67108864 | bytes 1048064 | tf_op jit(solution)/shard_map/convolution.6
  117.4 7.8 %fusion.4 = bf16[8192,512]{0,1:T(8,128)(2,1)} fusion(bf16[256,8192]{1,0:T(8,128)(2,1)} %param.18, bf16[256,256]{1,0:T(8,128)(2,1)S(1)} %fusion.26, bf16[256,256]{1,0:T(8,128)(2,1)S(1)} %get-tuple-element.225), kind=kOutput, calls=%fused_computation.17 | convolution fusion | flops 2152202240 | bytes 12845056 | tf_op jit(solution)/shard_map/dot_general | solution.py:87
  125.3 206.3 %reduce-scatter.3.cloned.1.call-done = bf16[256,512]{0,1:T(8,128)(2,1)} async-done(((bf16[8192,512]{0,1:T(8,128)(2,1)}), bf16[256,512]{0,1:T(8,128)(2,1)}) %reduce-scatter.3.cloned.1.call-update) | async-done | bytes 262160 | tf_op jit(solution)/shard_map/reduce_scatter | solution.py:86
  331.5 1.0 convert_element_type.66
  332.5 1.0 multiply_convert_fusion
  333.5 0.7 pad_maximum_fusion.3
  334.5 63.1 %all-gather.8.cloned.1.call-done = bf16[8192,512]{0,1:T(8,128)(2,1)} async-done(((bf16[256,512]{0,1:T(8,128)(2,1)}), bf16[8192,512]{0,1:T(8,128)(2,1)}) %all-gather.8.cloned.1.call-update) | async-done | bytes 8388624 | tf_op jit(solution)/shard_map/all_gather | solution.py:104
  397.6 6.9 %convolution_bitcast_fusion.2 = f32[256,512]{0,1:T(8,128)S(1)} fusion(bf16[8192,512]{0,1:T(8,128)(2,1)} %all-gather.8.cloned.1.call-done, bf16[256,8192]{1,0:T(8,128)(2,1)} %param.18), kind=kOutput, calls=%fused_computation.18 | convolution fusion | flops 2147483648 | bytes 13107200 | tf_op jit(solution)/shard_map/dot_general | solution.py:102
  404.9 1.5 broadcast_in_dim.21
  406.4 15.5 %while.25 = (s32[]{:T(128)}, bf16[2048,512]{1,0:T(8,128)(2,1)}, s32[]{:T(128)}, s32[]{:T(128)}, bf16[2304,256]{1,0:T(8,128)(2,1)S(1)}, /*index=5*/bf16[2,256,256...) while((s32[]{:T(128)}, bf16[2048,512]{1,0:T(8,128)(2,1)}, ...), condition=%wide.region_4.0_spmd, body=%wide.region_3.0_spmd.sunk | while | flops 67633160 | bytes 3406569 | solution.py:118
  406.4 13.6 %convolution_bitcast_fusion.6 = bf16[2,1,256,256]{3,1,0,2:T(2,128)(2,1)S(1)} fusion(bf16[256,1,256,2]{2,3,0,1:T(2,128)(2,1)S(1)} %bitcast.129, bf16[1,511,256,1]{2,1,3,0:T(8,128)(2,1)S(1)} %dynamic-slice_bitcast_fusion.5), kind=kOutput, calls=%fused_computation.8.clone.1 | convolution fusion | flops 67108864 | bytes 785920 | tf_op jit(solution)/shard_map/convolution.7
  421.1 0.7 maximum_dynamic-update-slice_fusion.2
  421.9 148.9 %reduce-scatter.5.cloned.1.call-done = bf16[256,512]{1,0:T(8,128)(2,1)} async-done(((bf16[2048,512]{1,0:T(8,128)(2,1)}), bf16[256,512]{1,0:T(8,128)(2,1)}) %reduce-scatter.5.cloned.1.call-update) | async-done | bytes 262160 | tf_op jit(solution)/shard_map/reduce_scatter | solution.py:121
  570.7 1.8 fusion.40
  (47 shorter events, 4.1 us)
Async XLA Ops:
  7.2 22.2 %copy-start.1 = (bf16[256,256]{1,0:T(8,128)(2,1)S(1)}, bf16[256,256]{1,0:T(8,128)(2,1)}, u32[]{:S(2)}) copy-start(bf16[256,256]{1,0:T(8,128)(2,1)} %param.12) | copy-start | bytes 393220
  7.2 54.7 %all-gather.4.cloned.1.call-start = ((), (), s32[]{:S(2)}) async-start(), calls=%async_computation.3 | async-start | bytes 1179648 | tf_op jit(solution)/shard_map/all_gather | solution.py:52
  8.6 11.6 %collective-permute-start = (bf16[2,256]{1,0:T(2,128)(2,1)S(1)}, bf16[2,256]{1,0:T(2,128)(2,1)S(1)}, u32[]{:S(2)}, u32[]{:S(2)}) collective-permute-start(bf16[2,256]{1,0:T(2,128)(2,1)S(1)} %slice.125), channel_id=1, source_target_pairs={{0,32},{32,64},{64,96},{96,128},{128,160},{160,192},{192,224},{1,3... | collective-permute-start | bytes 3080 | tf_op jit(solution)/shard_map/ppermute | solution.py:11
  13.1 7.1 %collective-permute-start.1 = (bf16[2,256]{1,0:T(2,128)(2,1)S(1)}, bf16[2,256]{1,0:T(2,128)(2,1)S(1)}, u32[]{:S(2)}, u32[]{:S(2)}) collective-permute-start(bf16[2,256]{1,0:T(2,128)(2,1)S(1)} %slice.131), channel_id=1, source_target_pairs={{0,32},{32,64},{64,96},{96,128},{128,160},{160,192},{192,224},{1,3... | collective-permute-start | bytes 3080 | tf_op jit(solution)/shard_map/ppermute | solution.py:11
  21.5 40.3 %all-to-all-start = ((bf16[8,256,256]{2,1,0:T(8,128)(2,1)}), bf16[8,256,256]{2,1,0:T(8,128)(2,1)S(1)}, u32[]{:S(2)}, u32[]{:S(2)}) async-start(bf16[8,256,256]{2,1,0:T(8,128)(2,1)} %tile.2), calls=%async_computation | async-start | bytes 2097152 | tf_op jit(solution)/shard_map/all_to_all | solution.py:63
  28.6 72.7 %all-gather.6.cloned.1.call-start = ((), (), s32[]{:S(2)}) async-start(), calls=%async_computation.4 | async-start | bytes 1179648 | tf_op jit(solution)/shard_map/all_gather | solution.py:53
  29.3 302.2 %reduce-scatter.3.cloned.1.call-start = ((), (), s32[]{:S(2)}) async-start(), calls=%async_computation.5 | async-start | bytes 8650752 | tf_op jit(solution)/shard_map/reduce_scatter | solution.py:86
  29.4 26.8 %collective-permute-start.2 = (bf16[2,256]{1,0:T(2,128)(2,1)S(1)}, bf16[2,256]{1,0:T(2,128)(2,1)S(1)}, u32[]{:S(2)}, u32[]{:S(2)}) collective-permute-start(bf16[2,256]{1,0:T(2,128)(2,1)S(1)} %slice.137), channel_id=1, source_target_pairs={{0,32},{32,64},{64,96},{96,128},{128,160},{160,192},{192,224},{1,3... | collective-permute-start | bytes 3080 | tf_op jit(solution)/shard_map/ppermute | solution.py:11
  101.5 15.7 %copy-start = (f32[256,256]{1,0:T(8,128)S(1)}, f32[256,256]{1,0:T(8,128)}, u32[]{:S(2)}) copy-start(f32[256,256]{1,0:T(8,128)} %convert_element_type.60) | copy-start | bytes 786436
  101.5 15.7 %copy-start.2 = (f32[2,256]{1,0:T(2,128)S(1)}, f32[2,256]{1,0:T(2,128)}, u32[]{:S(2)}) copy-start(f32[2,256]{1,0:T(2,128)} %convert_element_type.61) | copy-start | bytes 6148
  101.5 15.7 %copy-start.3 = (f32[1,1,256]{2,1,0:T(1,128)S(1)}, f32[1,1,256]{2,1,0:T(1,128)}, u32[]{:S(2)}) copy-start(f32[1,1,256]{2,1,0:T(1,128)} %get-tuple-element.237) | copy-start | bytes 3076
  101.5 15.7 %copy-start.4 = (f32[1,1,256]{2,1,0:T(1,128)S(1)}, f32[1,1,256]{2,1,0:T(1,128)}, u32[]{:S(2)}) copy-start(f32[1,1,256]{2,1,0:T(1,128)} %get-tuple-element.244) | copy-start | bytes 3076
  101.5 15.7 %copy-start.5 = (f32[1,1,256]{2,1,0:T(1,128)S(1)}, f32[1,1,256]{2,1,0:T(1,128)}, u32[]{:S(2)}) copy-start(f32[1,1,256]{2,1,0:T(1,128)} %get-tuple-element.245) | copy-start | bytes 3076
  125.2 272.4 %all-gather.8.cloned.1.call-start = ((), (), s32[]{:S(2)}) async-start(), calls=%async_computation.6 | async-start | bytes 8650752 | tf_op jit(solution)/shard_map/all_gather | solution.py:104
  334.3 236.5 %reduce-scatter.5.cloned.1.call-start = ((), (), s32[]{:S(2)}) async-start(), calls=%async_computation.7 | async-start | bytes 2359296 | tf_op jit(solution)/shard_map/reduce_scatter | solution.py:121
Sparse Core Ops, SparseCore 0:
  9.8 48.7 all-gather.3
  60.3 40.9 all-gather.5
  125.3 206.1 reduce-scatter.2
  334.4 63.1 all-gather.7
  422.0 148.7 reduce-scatter.4
